TPU v7x, 512 devices: a whole 4x8x8 slice. The times are simulated.
512 devices in a mesh: tm: 32 (over y, z_lo), row: 16 (over x, z_hi, core).
Axes of the slice: x: 4, y: 8, z: 8 (z_hi: 2, z_lo: 4; z = z_hi * 4 + z_lo), core: 2. Of those that a mesh axis runs over, the one named last changes fastest.
Arguments:
- latents: bfloat16 [64, 96, 80, 256], P('tm', 'row'), may hold values from -6 to 6
- conv_weight: bfloat16 [3, 3, 768, 256], replicated, may hold values from -0.078125 to 0.078125
- norm_gain: float32 [256], replicated, may hold values from 0.1 to 1.9
- depth_target: bfloat16 [64, 96, 80, 128], P('tm', 'row'), may hold values from -6 to 6
Outputs:
- features: bfloat16 [64, 96, 80, 256], P('tm', 'row')
- gram: float32 [256, 256], replicated
- cross: float32 [256, 128], replicated
All inputs are finite; a program needn't handle non-finite values.
Results may differ from a plain program's by a relative error of at most 0.003.
Values may be sent and summed in bfloat16 or wider, within the bound.
A program may use at most 64 MiB of HBM per device.

v0:
```python
import jax
import jax.numpy as jnp
from jax import lax
from jax.sharding import PartitionSpec as P


def from_behind(value, axis, steps):
    count = lax.axis_size(axis)
    first, last = (max(0, -steps), min(count, count - steps))
    return lax.ppermute(value, axis, [(source, source + steps) for source in range(first, last)])


def extended(cells, sides, width):
    for axis, dim in sides:
        count = lax.axis_size(axis)
        ends = count - 1
        head = lax.slice_in_dim(cells, 0, width, axis=dim)
        tail = lax.slice_in_dim(cells, cells.shape[dim] - width, cells.shape[dim], axis=dim)
        cells = jnp.concatenate(
            [
                lax.ppermute(tail, axis, [(i, (i + 1) % count) for i in range(ends)]),
                cells,
                lax.ppermute(head, axis, [((i + 1) % count, i) for i in range(ends)]),
            ],
            axis=dim,
        )
    return cells


def convolve(padded, conv_weight):
    frames = padded.shape[0] - 2
    rows = padded.shape[1] - 2
    cols = padded.shape[2]
    chans = conv_weight.shape[3]
    wide = jnp.pad(padded, ((0, 0), (0, 0), (1, 1), (0, 0)))
    stacked = jnp.concatenate(
        [wide[:, :, 0:cols], wide[:, :, 1 : cols + 1], wide[:, :, 2 : cols + 2]], axis=3
    )
    total = jnp.zeros((frames * rows * cols, chans), jnp.float32)
    for dtime in range(3):
        for drow in range(3):
            piece = stacked[dtime : dtime + frames, drow : drow + rows].reshape(
                frames * rows * cols, -1
            )
            total = total + jnp.dot(
                piece, conv_weight[dtime, drow], preferred_element_type=jnp.float32
            )
    return total


def on_device(latents, conv_weight, norm_gain, depth_target):
    cached = from_behind(latents, "tm", 1)
    joined = jnp.concatenate([cached, latents], axis=0)
    padded = extended(joined, (("row", 1),), 1)
    conv = convolve(padded, conv_weight)
    flat_in = latents.reshape(conv.shape[0], conv.shape[1]).astype(jnp.float32)
    normed = conv * jax.lax.rsqrt(jnp.mean(conv * conv, axis=1, keepdims=True) + 1e-06) * norm_gain
    flat = (flat_in + jax.nn.silu(normed)).astype(jnp.bfloat16)
    targets = depth_target.reshape(flat.shape[0], -1)
    gram_part = jnp.dot(flat.T, flat, preferred_element_type=jnp.float32)
    cross_part = jnp.dot(flat.T, targets, preferred_element_type=jnp.float32)
    count = flat.shape[0] * lax.axis_size("tm") * lax.axis_size("row")
    gram_sum, cross_sum = lax.psum((gram_part, cross_part), ("tm", "row"))
    return (flat.reshape(latents.shape), gram_sum / count, cross_sum / count)


def solution(mesh):
    in_specs = (P("tm", "row", None, None), P(), P(), P("tm", "row", None, None))
    out_specs = (P("tm", "row", None, None), P(), P())
    return jax.shard_map(
        on_device, mesh=mesh, in_specs=in_specs, out_specs=out_specs, check_vma=False
    )
```

profile of v0, /device:TPU:1, one launch (start us, length us, event | category | flops | bytes accessed | tf_op | source)
XLA Modules:
  0.0 338.9 jit_solution(941491397047165075)
XLA Ops:
  7.2 0.0 copy-start
  7.2 0.0 all-reduce.4.cloned.1.call-start
  7.2 5.0 %collective-permute-start = (bf16[2,6,80,256]{3,2,1,0:T(8,128)(2,1)}, bf16[2,6,80,256]{3,2,1,0:T(8,128)(2,1)S(1)}, u32[]{:S(2)}, u32[]{:S(2)}) collective-permute-start(bf16[2,6,80,256]{3,2,1,0:T(8,128)(2,1)} %param.4), channel_id=1, source_target_pairs={{0,16},{16,32},{32,48},{48,64},{64,80},{80,96},{96,112},{112,128},... | collective-permute-start | bytes 1474568 | tf_op jit(solution)/shard_map/ppermute | solution.py:10
  12.2 7.8 %collective-permute-done = bf16[2,6,80,256]{3,2,1,0:T(8,128)(2,1)S(1)} collective-permute-done((bf16[2,6,80,256]{3,2,1,0:T(8,128)(2,1)}, bf16[2,6,80,256]{3,2,1,0:T(8,128)(2,1)S(1)}, u32[]{:S(2)}, u32[]{:S(2)}) %collective-permute-start) | collective-permute-done | bytes 491552 | tf_op jit(solution)/shard_map/ppermute | solution.py:10
  20.1 1.1 constant_dynamic-update-slice_fusion
  21.2 13.5 %collective-permute-start.1 = (bf16[4,1,80,256]{3,2,1,0:T(8,128)(2,1)S(1)}, bf16[4,1,80,256]{3,2,1,0:T(8,128)(2,1)S(1)}, u32[]{:S(2)}, u32[]{:S(2)}) collective-permute-start(bf16[4,1,80,256]{3,2,1,0:T(8,128)(2,1)S(1)} %get-tuple-element.16), channel_id=1, source_target_pairs={{0,1},{1,2},{2,3},{3,4},{4,5},{5,6},{6,7},{7,8},{8,9},{9,10},{10,1... | collective-permute-start | bytes 491528 | tf_op jit(solution)/shard_map/ppermute | solution.py:21
  34.7 1.9 collective-permute-start.2
  36.6 2.1 collective-permute-done.1
  38.7 7.3 %collective-permute-done.2 = bf16[4,1,80,256]{3,2,1,0:T(8,128)(2,1)S(1)} collective-permute-done((bf16[4,1,80,256]{3,2,1,0:T(8,128)(2,1)S(1)}, bf16[4,1,80,256]{3,2,1,0:T(8,128)(2,1)S(1)}, u32[]{:S(2)}, u32[]{:S(2)}) %collective-permute-start.2) | collective-permute-done | bytes 163872 | tf_op jit(solution)/shard_map/ppermute | solution.py:23
  46.0 0.8 fusion.5
  46.7 0.9 fusion.41
  47.6 0.3 pad_maximum_fusion
  48.0 0.0 copy-start.1
  48.0 1.2 fusion.40
  49.2 0.7 copy-done.1
  50.0 0.5 fusion.14
  50.5 0.5 fusion.16
  51.1 0.5 fusion.18
  51.6 0.5 fusion.20
  52.2 0.5 fusion.22
  52.8 0.5 fusion.24
  53.3 0.5 fusion.26
  53.9 0.5 fusion.28
  54.4 0.0 copy-start.2
  54.4 0.0 copy-start.4
  54.5 0.9 multiply_reduce_fusion
  55.4 0.1 copy-done.2
  55.5 0.0 copy-done.4
  55.5 0.4 fusion.13
  55.9 0.0 copy-start.3
  55.9 1.1 fusion.43
  56.9 0.0 copy-done
  56.9 1.0 fusion.44
  57.9 0.0 all-reduce.4.cloned.1.call-update
  58.0 270.9 %all-reduce.4.cloned.1.call-done = (f32[256,256]{1,0:T(8,128)}, f32[256,128]{1,0:T(8,128)}) async-done(((f32[256,256]{1,0:T(8,128)}, f32[256,128]{1,0:T(8,128)}), (f32[256,256]{1,0:T(8,128)}, f32[256,128]{1,0:T(8,128)})) %all-reduce.4.cloned.1.call-update) | async-done | bytes 393232 | tf_op jit(solution)/shard_map/psum | solution.py:63
  328.8 1.7 broadcast_multiply_fusion
  330.5 0.0 copy-done.3
  330.5 1.6 broadcast_multiply_fusion.1
  (3 shorter events, 0.1 us)
Async XLA Ops:
  7.2 49.8 %copy-start = (bf16[2,6,80,128]{3,2,1,0:T(8,128)(2,1)S(1)}, bf16[2,6,80,128]{3,2,1,0:T(8,128)(2,1)}, u32[]{:S(2)}) copy-start(bf16[2,6,80,128]{3,2,1,0:T(8,128)(2,1)} %param.7) | copy-start | bytes 737284
  7.2 321.6 %all-reduce.4.cloned.1.call-start = ((), (), s32[]{:S(2)}) async-start(), calls=%async_computation | async-start | bytes 786432 | tf_op jit(solution)/shard_map/psum | solution.py:63
  7.2 12.8 %collective-permute-start = (bf16[2,6,80,256]{3,2,1,0:T(8,128)(2,1)}, bf16[2,6,80,256]{3,2,1,0:T(8,128)(2,1)S(1)}, u32[]{:S(2)}, u32[]{:S(2)}) collective-permute-start(bf16[2,6,80,256]{3,2,1,0:T(8,128)(2,1)} %param.4), channel_id=1, source_target_pairs={{0,16},{16,32},{32,48},{48,64},{64,80},{80,96},{96,112},{112,128},... | collective-permute-start | bytes 1474568 | tf_op jit(solution)/shard_map/ppermute | solution.py:10
  21.2 17.5 %collective-permute-start.1 = (bf16[4,1,80,256]{3,2,1,0:T(8,128)(2,1)S(1)}, bf16[4,1,80,256]{3,2,1,0:T(8,128)(2,1)S(1)}, u32[]{:S(2)}, u32[]{:S(2)}) collective-permute-start(bf16[4,1,80,256]{3,2,1,0:T(8,128)(2,1)S(1)} %get-tuple-element.16), channel_id=1, source_target_pairs={{0,1},{1,2},{2,3},{3,4},{4,5},{5,6},{6,7},{7,8},{8,9},{9,10},{10,1... | collective-permute-start | bytes 491528 | tf_op jit(solution)/shard_map/ppermute | solution.py:21
  34.7 11.3 %collective-permute-start.2 = (bf16[4,1,80,256]{3,2,1,0:T(8,128)(2,1)S(1)}, bf16[4,1,80,256]{3,2,1,0:T(8,128)(2,1)S(1)}, u32[]{:S(2)}, u32[]{:S(2)}) collective-permute-start(bf16[4,1,80,256]{3,2,1,0:T(8,128)(2,1)S(1)} %get-tuple-element.17), channel_id=1, source_target_pairs={{1,0},{2,1},{3,2},{4,3},{5,4},{6,5},{7,6},{8,7},{9,8},{10,9},{11,1... | collective-permute-start | bytes 491528 | tf_op jit(solution)/shard_map/ppermute | solution.py:23
  48.0 2.0 copy-start.1
  54.4 1.0 copy-start.2
  54.4 1.0 copy-start.4
  55.9 274.6 %copy-start.3 = (bf16[960,256]{1,0:T(8,128)(2,1)}, bf16[960,256]{1,0:T(8,128)(2,1)S(1)}, u32[]{:S(2)}) copy-start(bf16[960,256]{1,0:T(8,128)(2,1)S(1)} %fusion.13) | copy-start | bytes 1474564
Sparse Core Ops, SparseCore 0:
  58.1 270.6 all-reduce.3
where the time goes:
time: 339 us
  waiting for transfers between devices  288 us (85%)
  starting transfers between devices  20.4 us (6%)
  between operations  14.2 us (4%)
  matrix products  7.34 us (2%)
  other arithmetic  4.74 us (1%)
  local copies, waits for them, and re-layouts  4.12 us (1%)
    psum x1, waiting for transfers between devices, on_device(): gram_sum, cross_sum = lax.psum((gram_part, cross_part), ('tm', 'row'))  271 us
    ppermute x1, starting transfers between devices, extended(): lax.ppermute(tail, axis, [(i, (i + 1) % count) for i in range(ends)])  13.5 us
    ppermute x1, waiting for transfers between devices, from_behind(): lax.ppermute(value, axis, [(source, source + steps) for source in range(f...  7.81 us
    ppermute x1, waiting for transfers between devices, extended(): lax.ppermute(head, axis, [((i + 1) % count, i) for i in range(ends)])  7.3 us
  transfers between devices with their start and end apart: 4, of which 4 were waited for; matrix products, arithmetic and copies ran while one was open for 0% of the time, Pallas kernels for 0%

commit v1 on v0

--- a/solution.py
+++ b/solution.py
@@ -1,7 +1,139 @@
+import functools
+
 import jax
 import jax.numpy as jnp
 from jax import lax
+from jax.experimental import pallas as pl
+from jax.experimental.pallas import tpu as pltpu
 from jax.sharding import PartitionSpec as P
+
+MESH = pl.DeviceIdType.MESH
+FAR = (4, 3, 5, 2, 6, 1, 7)
+
+
+def reduce_kernel(scale, g_ref, c_ref, gram_ref, cross_ref, pay, rs, ya, za, yb, zb, fin, send_sem, recv_sem):
+    tm = lax.axis_index("tm")
+    row = lax.axis_index("row")
+    y, zl = tm // 4, tm % 4
+    x, zh, core = row // 4, (row // 2) % 2, row % 2
+
+    def a_peer(j):
+        return tm, (j // 2) * 4 + zh * 2 + j % 2
+
+    def y_peer(j):
+        return j * 4 + zl, row
+
+    def z_peer(j):
+        return y * 4 + j % 4, x * 4 + (j // 4) * 2 + core
+
+    a_me, y_me, z_me = x * 2 + core, y, zh * 4 + zl
+    groups = ((a_me, a_peer), (y_me, y_peer), (z_me, z_peer))
+
+    barrier = pltpu.get_barrier_semaphore()
+    for me, peer in groups:
+        for k in range(1, 8):
+            pl.semaphore_signal(barrier, inc=1, device_id=peer((me + k) % 8), device_id_type=MESH)
+    pay[0:128] = g_ref[0:128, 0:128]
+    pay[128:256] = g_ref[0:128, 128:256]
+    pay[256:384] = g_ref[128:256, 128:256]
+    pay[384:640] = c_ref[...]
+    pl.semaphore_wait(barrier, 21)
+
+    def copy(stage, me, peer, k, src, dst):
+        j = (me + k) % 8
+        return pltpu.make_async_remote_copy(
+            src_ref=src(j), dst_ref=dst(me), send_sem=send_sem.at[stage, j], recv_sem=recv_sem.at[stage, me],
+            device_id=peer(j), device_id_type=MESH,
+        )
+
+    def arrival(stage, me, peer, k, src, dst):
+        j = (me + k) % 8
+        return pltpu.make_async_remote_copy(
+            src_ref=src(j), dst_ref=dst(j), send_sem=send_sem.at[stage, j], recv_sem=recv_sem.at[stage, j],
+            device_id=peer(j), device_id_type=MESH,
+        )
+
+    def send(stage, me, peer, src, dst):
+        for k in FAR:
+            copy(stage, me, peer, k, src, dst).start()
+
+    def receive(stage, me, peer, src, dst):
+        for k in FAR:
+            arrival(stage, me, peer, k, src, dst).wait_recv()
+
+    def drain(stage, me, peer, src, dst):
+        for k in FAR:
+            copy(stage, me, peer, k, src, dst).wait_send()
+
+    def chunk(ref):
+        return lambda j: ref.at[pl.ds(pl.multiple_of(j * 80, 8), 80)]
+
+    def slot(ref):
+        return lambda j: ref.at[j]
+
+    def total(ref):
+        acc = ref[0]
+        for j in range(1, 8):
+            acc = acc + ref[j]
+        return acc
+
+    s0 = (0, a_me, a_peer, chunk(pay), slot(rs))
+    send(*s0)
+    rs[a_me] = pay[pl.ds(pl.multiple_of(a_me * 80, 8), 80)]
+    receive(*s0)
+    part = total(rs)
+    ya[y_me] = part[0:40]
+    za[z_me] = part[40:80]
+    s1 = (1, y_me, y_peer, lambda j: ya.at[y_me], slot(ya))
+    s2 = (2, z_me, z_peer, lambda j: za.at[z_me], slot(za))
+    send(*s1)
+    send(*s2)
+    receive(*s1)
+    zb[z_me] = total(ya)
+    s3 = (3, z_me, z_peer, lambda j: zb.at[z_me], slot(zb))
+    send(*s3)
+    receive(*s2)
+    yb[y_me] = total(za)
+    s4 = (4, y_me, y_peer, lambda j: yb.at[y_me], slot(yb))
+    send(*s4)
+    receive(*s3)
+    here = pl.multiple_of(a_me * 80, 8)
+    fin[pl.ds(here, 40)] = total(zb)
+    receive(*s4)
+    fin[pl.ds(here + 40, 40)] = total(yb)
+    s5 = (5, a_me, a_peer, lambda j: fin.at[pl.ds(here, 80)], chunk(fin))
+    send(*s5)
+    receive(*s5)
+    gram_ref[0:128, 0:128] = fin[0:128] * scale
+    gram_ref[0:128, 128:256] = fin[128:256] * scale
+    gram_ref[128:256, 0:128] = fin[128:256].T * scale
+    gram_ref[128:256, 128:256] = fin[256:384] * scale
+    cross_ref[...] = fin[384:640] * scale
+    for s in (s0, s1, s2, s3, s4, s5):
+        drain(*s)
+
+
+def reduce_all(gram, cross, count):
+    vmem = pl.BlockSpec(memory_space=pltpu.VMEM)
+    f32 = jnp.float32
+    return pl.pallas_call(
+        functools.partial(reduce_kernel, 1.0 / count),
+        out_shape=(jax.ShapeDtypeStruct((256, 256), f32), jax.ShapeDtypeStruct((256, 128), f32)),
+        in_specs=[vmem, vmem],
+        out_specs=(vmem, vmem),
+        scratch_shapes=[
+            pltpu.VMEM((640, 128), f32),
+            pltpu.VMEM((8, 80, 128), f32),
+            pltpu.VMEM((8, 40, 128), f32),
+            pltpu.VMEM((8, 40, 128), f32),
+            pltpu.VMEM((8, 40, 128), f32),
+            pltpu.VMEM((8, 40, 128), f32),
+            pltpu.VMEM((640, 128), f32),
+            pltpu.SemaphoreType.DMA((6, 8)),
+            pltpu.SemaphoreType.DMA((6, 8)),
+        ],
+        compiler_params=pltpu.CompilerParams(collective_id=0, has_side_effects=True),
+    )(gram, cross)
 
 
 def from_behind(value, axis, steps):
@@ -60,8 +192,8 @@
     gram_part = jnp.dot(flat.T, flat, preferred_element_type=jnp.float32)
     cross_part = jnp.dot(flat.T, targets, preferred_element_type=jnp.float32)
     count = flat.shape[0] * lax.axis_size("tm") * lax.axis_size("row")
-    gram_sum, cross_sum = lax.psum((gram_part, cross_part), ("tm", "row"))
-    return (flat.reshape(latents.shape), gram_sum / count, cross_sum / count)
+    gram, cross = reduce_all(gram_part, cross_part, count)
+    return (flat.reshape(latents.shape), gram, cross)
 
 
 def solution(mesh):

time: 339 us -> 90.2 us (0.27)
  waiting for transfers between devices: 288 us -> 17.2 us
  Pallas kernels: 0 us -> 35.2 us
  between operations: 14.2 us -> 0.82 us
    psum x1 -> x0, waiting for transfers between devices: 271 us -> none  [on_device(): gram_sum, cross_sum = lax.psum((gram_part, cross_part), ('tm', 'row'))]
    pallas_call x0 -> x1, Pallas kernels: none -> 35.2 us  [reduce_all(): pl.pallas_call(functools.partial(reduce_kernel, 1.0 / count), out_shape=(...]
  transfers between devices with their start and end apart: 4 -> 3, of which waited for: 4 -> 3; matrix products, arithmetic and copies ran while one was open for 0% -> 0% of each run, Pallas kernels for 0% -> 0%
where the time goes in v1:
time: 90.2 us; the launch traced here: 89.8 us
  Pallas kernels  35.2 us (39%)
  starting transfers between devices  20.4 us (23%)
  waiting for transfers between devices  17.2 us (19%)
  local copies, waits for them, and re-layouts  7.36 us (8%)
  matrix products  7.34 us (8%)
  other arithmetic  1.49 us (2%)
    pallas_call x1, Pallas kernels, reduce_all(): pl.pallas_call(functools.partial(reduce_kernel, 1.0 / count), out_shape=(...  35.2 us
    ppermute x1, starting transfers between devices, extended(): lax.ppermute(tail, axis, [(i, (i + 1) % count) for i in range(ends)])  13.5 us
    ppermute x1, waiting for transfers between devices, from_behind(): lax.ppermute(value, axis, [(source, source + steps) for source in range(f...  7.81 us
    ppermute x1, waiting for transfers between devices, extended(): lax.ppermute(head, axis, [((i + 1) % count, i) for i in range(ends)])  7.3 us
    dot_general x9, matrix products, convolve(): jnp.dot(piece, conv_weight[dtime, drow], preferred_element_type=jnp.float32)  5.29 us
    ppermute x1, starting transfers between devices, from_behind(): lax.ppermute(value, axis, [(source, source + steps) for source in range(f...  4.98 us
    unnamed x13, local copies, waits for them, and re-layouts  4.13 us
    ppermute x1, waiting for transfers between devices, extended(): lax.ppermute(tail, axis, [(i, (i + 1) % count) for i in range(ends)])  2.07 us
  transfers between devices with their start and end apart: 3, of which 3 were waited for; matrix products, arithmetic and copies ran while one was open for 0% of the time, Pallas kernels for 0%

profile of v1, /device:TPU:1, one launch (start us, length us, event | category | flops | bytes accessed | tf_op | source)
XLA Modules:
  0.0 89.8 jit_solution(259356992491585565)
XLA Ops:
  0.6 0.0 copy-start
  0.6 5.0 %collective-permute-start = (bf16[2,6,80,256]{3,2,1,0:T(8,128)(2,1)}, bf16[2,6,80,256]{3,2,1,0:T(8,128)(2,1)S(1)}, u32[]{:S(2)}, u32[]{:S(2)}) collective-permute-start(bf16[2,6,80,256]{3,2,1,0:T(8,128)(2,1)} %param.4), channel_id=1, source_target_pairs={{0,16},{16,32},{32,48},{48,64},{64,80},{80,96},{96,112},{112,128},... | collective-permute-start | bytes 1474568 | tf_op jit(solution)/shard_map/ppermute | solution.py:142
  5.6 7.8 %collective-permute-done = bf16[2,6,80,256]{3,2,1,0:T(8,128)(2,1)S(1)} collective-permute-done((bf16[2,6,80,256]{3,2,1,0:T(8,128)(2,1)}, bf16[2,6,80,256]{3,2,1,0:T(8,128)(2,1)S(1)}, u32[]{:S(2)}, u32[]{:S(2)}) %collective-permute-start) | collective-permute-done | bytes 491552 | tf_op jit(solution)/shard_map/ppermute | solution.py:142
  13.5 1.1 %constant_dynamic-update-slice_fusion = bf16[4,6,80,256]{3,2,1,0:T(8,128)(2,1)S(1)} fusion(bf16[4,6,80,256]{3,2,1,0:T(8,128)(2,1)S(1)} %constant_dynamic-update-slice_fusion.1, bf16[2,6,80,256]{3,2,1,0:T(8,128)(2,1)} %param.4), kind=kLoop, calls=%fused_computation.46 | loop fusion | bytes 983040 | tf_op jit(solution)/shard_map/concatenate | solution.py:185
  14.6 13.5 %collective-permute-start.1 = (bf16[4,1,80,256]{3,2,1,0:T(8,128)(2,1)S(1)}, bf16[4,1,80,256]{3,2,1,0:T(8,128)(2,1)S(1)}, u32[]{:S(2)}, u32[]{:S(2)}) collective-permute-start(bf16[4,1,80,256]{3,2,1,0:T(8,128)(2,1)S(1)} %get-tuple-element.18), channel_id=1, source_target_pairs={{0,1},{1,2},{2,3},{3,4},{4,5},{5,6},{6,7},{7,8},{8,9},{9,10},{10,1... | collective-permute-start | bytes 491528 | tf_op jit(solution)/shard_map/ppermute | solution.py:153
  28.1 1.9 %collective-permute-start.2 = (bf16[4,1,80,256]{3,2,1,0:T(8,128)(2,1)S(1)}, bf16[4,1,80,256]{3,2,1,0:T(8,128)(2,1)S(1)}, u32[]{:S(2)}, u32[]{:S(2)}) collective-permute-start(bf16[4,1,80,256]{3,2,1,0:T(8,128)(2,1)S(1)} %get-tuple-element.19), channel_id=1, source_target_pairs={{1,0},{2,1},{3,2},{4,3},{5,4},{6,5},{7,6},{8,7},{9,8},{10,9},{11,1... | collective-permute-start | bytes 491528 | tf_op jit(solution)/shard_map/ppermute | solution.py:155
  30.0 2.1 %collective-permute-done.1 = bf16[4,1,80,256]{3,2,1,0:T(8,128)(2,1)S(1)} collective-permute-done((bf16[4,1,80,256]{3,2,1,0:T(8,128)(2,1)S(1)}, bf16[4,1,80,256]{3,2,1,0:T(8,128)(2,1)S(1)}, u32[]{:S(2)}, u32[]{:S(2)}) %collective-permute-start.1) | collective-permute-done | bytes 163872 | tf_op jit(solution)/shard_map/ppermute | solution.py:153
  32.1 7.3 %collective-permute-done.2 = bf16[4,1,80,256]{3,2,1,0:T(8,128)(2,1)S(1)} collective-permute-done((bf16[4,1,80,256]{3,2,1,0:T(8,128)(2,1)S(1)}, bf16[4,1,80,256]{3,2,1,0:T(8,128)(2,1)S(1)}, u32[]{:S(2)}, u32[]{:S(2)}) %collective-permute-start.2) | collective-permute-done | bytes 163872 | tf_op jit(solution)/shard_map/ppermute | solution.py:155
  39.4 0.8 fusion.5
  40.2 0.9 fusion.41
  41.1 0.3 pad_maximum_fusion
  41.4 0.0 copy-start.1
  41.4 1.2 %fusion.40 = (bf16[2,6,80,768]{3,2,1,0:T(8,128)(2,1)S(1)}, bf16[2,6,80,768]{3,2,1,0:T(8,128)(2,1)S(1)}, bf16[2,6,80,768]{3,2,1,0:T(8,128)(2,1)S(1)}, bf16[2,6,80...) fusion(bf16[4,8,80,768]{3,2,1,0:T(8,128)(2,1)S(1)} %pad_maximum, ...), kind=kLoop, calls=%fused_computation.49 | loop fusion | bytes 26542080 | tf_op jit(solution)/shard_map/slice | solution.py:174
  42.7 0.7 copy-done.1
  43.4 0.5 fusion.14
  43.9 0.5 fusion.16
  44.5 0.5 fusion.18
  45.1 0.5 fusion.20
  45.6 0.5 fusion.22
  46.2 0.5 fusion.24
  46.7 0.5 fusion.26
  47.3 0.5 fusion.28
  47.8 0.0 copy-start.2
  47.9 0.0 copy-start.4
  47.9 0.9 %multiply_reduce_fusion = (f32[960]{0:T(1024)S(1)}, f32[960,256]{1,0:T(8,128)S(1)}) fusion(f32[960,256]{1,0:T(8,128)S(1)} %fusion.14, f32[960,256]{1,0:T(8,128)S(1)} %fusion.16, f32[960,256]{1,0:T(8,128)S(1)} %fusion.18, f32[960,256]{1,0:T(8,128)S(1)} %fusion.20, f32[960,256]{1,0:T(8,128)S(1)} %fusion.22, f32[960,256]{1,0:T(8,128)S(1)} %fusion.24, ...), kind=kOutput, calls=%fused_computation.19 | convolution fusion | flops 379944000 | bytes 10718976 | tf_op jit(solution)/shard_map/dot_general | solution.py:177
  48.8 0.1 copy-done.2
  48.9 0.0 copy-done.4
  48.9 0.4 fusion.13
  49.3 0.0 copy-start.3
  49.3 1.0 %fusion.43.g_ref = f32[256,256]{1,0:T(8,128)} fusion(bf16[960,256]{1,0:T(8,128)(2,1)S(1)} %fusion.13), kind=kOutput, calls=%fused_computation.52 | convolution fusion | flops 125829120 | bytes 753664 | tf_op jit(solution)/shard_map/dot_general | solution.py:192
  50.4 0.0 copy-done
  50.4 1.0 %fusion.44.c_ref = f32[256,128]{1,0:T(8,128)} fusion(bf16[960,256]{1,0:T(8,128)(2,1)S(1)} %fusion.13, bf16[960,128]{1,0:T(8,128)(2,1)S(1)} %bitcast.56), kind=kOutput, calls=%fused_computation.53 | convolution fusion | flops 62914560 | bytes 868352 | tf_op jit(solution)/shard_map/dot_general | solution.py:193
  51.3 35.2 %shard_map.67 = (f32[256,256]{1,0:T(8,128)}, f32[256,128]{1,0:T(8,128)}) custom-call(f32[256,256]{1,0:T(8,128)} %fusion.43.g_ref, f32[256,128]{1,0:T(8,128)} %fusion.44.c_ref), custom_call_target="tpu_custom_call" | custom-call | tf_op jit(solution)/shard_map/pallas_call | solution.py:119
  86.6 1.7 %copy.10 = f32[256,256]{1,0:T(8,128)} copy(f32[256,256]{1,0:T(8,128)} %get-tuple-element.26) | data formatting | bytes 524288
  88.2 0.0 copy-done.3
  88.2 1.6 %copy.11 = f32[256,128]{1,0:T(8,128)} copy(f32[256,128]{1,0:T(8,128)} %get-tuple-element.27) | data formatting | bytes 262144
  (3 shorter events, 0.1 us)
Async XLA Ops:
  0.6 49.7 %copy-start = (bf16[2,6,80,128]{3,2,1,0:T(8,128)(2,1)S(1)}, bf16[2,6,80,128]{3,2,1,0:T(8,128)(2,1)}, u32[]{:S(2)}) copy-start(bf16[2,6,80,128]{3,2,1,0:T(8,128)(2,1)} %param.7) | copy-start | bytes 737284
  0.6 12.8 %collective-permute-start = (bf16[2,6,80,256]{3,2,1,0:T(8,128)(2,1)}, bf16[2,6,80,256]{3,2,1,0:T(8,128)(2,1)S(1)}, u32[]{:S(2)}, u32[]{:S(2)}) collective-permute-start(bf16[2,6,80,256]{3,2,1,0:T(8,128)(2,1)} %param.4), channel_id=1, source_target_pairs={{0,16},{16,32},{32,48},{48,64},{64,80},{80,96},{96,112},{112,128},... | collective-permute-start | bytes 1474568 | tf_op jit(solution)/shard_map/ppermute | solution.py:142
  14.6 17.5 %collective-permute-start.1 = (bf16[4,1,80,256]{3,2,1,0:T(8,128)(2,1)S(1)}, bf16[4,1,80,256]{3,2,1,0:T(8,128)(2,1)S(1)}, u32[]{:S(2)}, u32[]{:S(2)}) collective-permute-start(bf16[4,1,80,256]{3,2,1,0:T(8,128)(2,1)S(1)} %get-tuple-element.18), channel_id=1, source_target_pairs={{0,1},{1,2},{2,3},{3,4},{4,5},{5,6},{6,7},{7,8},{8,9},{9,10},{10,1... | collective-permute-start | bytes 491528 | tf_op jit(solution)/shard_map/ppermute | solution.py:153
  28.1 11.3 %collective-permute-start.2 = (bf16[4,1,80,256]{3,2,1,0:T(8,128)(2,1)S(1)}, bf16[4,1,80,256]{3,2,1,0:T(8,128)(2,1)S(1)}, u32[]{:S(2)}, u32[]{:S(2)}) collective-permute-start(bf16[4,1,80,256]{3,2,1,0:T(8,128)(2,1)S(1)} %get-tuple-element.19), channel_id=1, source_target_pairs={{1,0},{2,1},{3,2},{4,3},{5,4},{6,5},{7,6},{8,7},{9,8},{10,9},{11,1... | collective-permute-start | bytes 491528 | tf_op jit(solution)/shard_map/ppermute | solution.py:155
  41.4 2.0 %copy-start.1 = (bf16[3,3,768,256]{3,2,1,0:T(8,128)(2,1)S(1)}, bf16[3,3,768,256]{3,2,1,0:T(8,128)(2,1)}, u32[]{:S(2)}) copy-start(bf16[3,3,768,256]{3,2,1,0:T(8,128)(2,1)} %param.5) | copy-start | bytes 10616836
  47.8 1.0 %copy-start.2 = (bf16[2,6,80,256]{3,2,1,0:T(8,128)(2,1)S(1)}, bf16[2,6,80,256]{3,2,1,0:T(8,128)(2,1)}, u32[]{:S(2)}) copy-start(bf16[2,6,80,256]{3,2,1,0:T(8,128)(2,1)} %param.4) | copy-start | bytes 1474564
  47.9 1.0 %copy-start.4 = (f32[256]{0:T(256)S(1)}, f32[256]{0:T(256)}, u32[]{:S(2)}) copy-start(f32[256]{0:T(256)} %param.6) | copy-start | bytes 3076
  49.3 38.9 %copy-start.3 = (bf16[960,256]{1,0:T(8,128)(2,1)}, bf16[960,256]{1,0:T(8,128)(2,1)S(1)}, u32[]{:S(2)}) copy-start(bf16[960,256]{1,0:T(8,128)(2,1)S(1)} %fusion.13) | copy-start | bytes 1474564

commit v2 on v1

v2 whole, which is shorter than its diff:
```python
import functools

import jax
import jax.numpy as jnp
from jax import lax
from jax.experimental import pallas as pl
from jax.experimental.pallas import tpu as pltpu
from jax.sharding import PartitionSpec as P

MESH = pl.DeviceIdType.MESH
FAR = (4, 3, 5, 2, 6, 1, 7)
F32, BF16 = jnp.float32, jnp.bfloat16
OWN = (((0, 2),), ((0, 1), (1, 2)))
NEXT = (((0, 0), (1, 1)), ((1, 0),))


def layer_kernel(
    lat_hbm, w_hbm, gain_ref, tgt_hbm, feat, fin,
    win, w, tgt, own, nxt, halo, conv_in, conv_edge, zin_out, zin, zed_out, zed,
    pay, rs, ya, za, yb, zb, load_sem, side_send, side_recv, z_send, z_recv, send_sem, recv_sem,
):
    tm = lax.axis_index("tm")
    row = lax.axis_index("row")
    y, zl = tm // 4, tm % 4
    x, zh, core = row // 4, (row // 2) % 2, row % 2

    def a_peer(j):
        return tm, (j // 2) * 4 + zh * 2 + j % 2

    def y_peer(j):
        return j * 4 + zl, row

    def z_peer(j):
        return y * 4 + j % 4, x * 4 + (j // 4) * 2 + core

    a_me, y_me, z_me = x * 2 + core, y, zh * 4 + zl
    has_prev, has_next, has_up, has_down = tm > 0, tm < 31, row > 0, row < 15

    barrier = pltpu.get_barrier_semaphore()
    near = ((has_prev, (tm - 1, row)), (has_next, (tm + 1, row)), (has_up, (tm, row - 1)), (has_down, (tm, row + 1)))
    expected = jnp.int32(21)
    for there, device in near:
        @pl.when(there)
        def _():
            pl.semaphore_signal(barrier, inc=1, device_id=device, device_id_type=MESH)
        expected = expected + there.astype(jnp.int32)
    for me, peer in ((a_me, a_peer), (y_me, y_peer), (z_me, z_peer)):
        for k in range(1, 8):
            pl.semaphore_signal(barrier, inc=1, device_id=peer((me + k) % 8), device_id_type=MESH)

    loads = [pltpu.make_async_copy(lat_hbm, win.at[:, 1:7], load_sem.at[0])]
    loads += [pltpu.make_async_copy(w_hbm.at[dt], w.at[dt], load_sem.at[1 + dt]) for dt in range(3)]
    loads += [pltpu.make_async_copy(tgt_hbm, tgt, load_sem.at[4])]
    for load in loads:
        load.start()
    blank = jnp.zeros((2, 80, 256), BF16)
    win[:, 0] = blank
    win[:, 7] = blank

    @pl.when(row == 0)
    def _():
        halo[0] = blank

    @pl.when(row == 15)
    def _():
        halo[1] = blank

    @pl.when(tm == 0)
    def _():
        zin[...] = jnp.zeros(zin.shape, BF16)
        zed[...] = jnp.zeros(zed.shape, BF16)

    def taps(dst, outs):
        @pl.loop(0, 3)
        def _(dw):
            cols = pl.ds(pl.multiple_of(dw * 256, 256), 256)
            for o, pairs in enumerate(outs):
                acc = None
                for frame, dt in pairs:
                    for dh in range(3):
                        piece = win[frame, dh : dh + 6].reshape(480, 256)
                        prod = jnp.dot(piece, w[dt, dh, cols], preferred_element_type=F32)
                        acc = prod if acc is None else acc + prod
                dst[o, dw] = acc

    def joined(src, o, rows, size):
        col = lax.broadcasted_iota(jnp.int32, (size, 1), 0) % 80
        left = jnp.where(col == 0, 0.0, pltpu.roll(src[o, 0, rows], 1, 0))
        right = jnp.where(col == 79, 0.0, pltpu.roll(src[o, 2, rows], size - 1, 0))
        return src[o, 1, rows] + left + right

    for load in loads[:3]:
        load.wait()
    taps(nxt, NEXT)
    for f in range(2):
        zin_out[f] = joined(nxt, f, pl.ds(80, 320), 320).astype(BF16).reshape(4, 80, 256)
    pl.semaphore_wait(barrier, expected)

    def side_copy(to):
        return pltpu.make_async_remote_copy(
            src_ref=win.at[:, 6 - 5 * to], dst_ref=halo.at[to], send_sem=side_send.at[to], recv_sem=side_recv.at[to],
            device_id=(tm, row + 1 - 2 * to), device_id_type=MESH,
        )

    def inner_copy(f):
        return pltpu.make_async_remote_copy(
            src_ref=zin_out.at[f], dst_ref=zin.at[f], send_sem=z_send.at[f], recv_sem=z_recv.at[f],
            device_id=(tm + 1, row), device_id_type=MESH,
        )

    def edge_copy(side):
        return pltpu.make_async_remote_copy(
            src_ref=zed_out.at[side], dst_ref=zed.at[side], send_sem=z_send.at[2 + side], recv_sem=z_recv.at[2 + side],
            device_id=(tm + 1, row), device_id_type=MESH,
        )

    @pl.when(has_down)
    def _():
        side_copy(0).start()

    @pl.when(has_up)
    def _():
        side_copy(1).start()

    @pl.when(has_next)
    def _():
        inner_copy(0).start()
        inner_copy(1).start()

    loads[3].wait()
    taps(own, OWN)
    for f in range(2):
        conv_in[f] = joined(own, f, pl.ds(80, 320), 320)

    def side_step(i, carry):
        side = (1 - core) * (1 - i) + core * i
        other = row + 2 * side - 1

        @pl.when((other >= 0) & (other <= 15))
        def _():
            side_copy(side).wait_recv()

        dh = 2 * side
        rows = pl.ds(pl.multiple_of(side * 400, 80), 80)

        @pl.loop(0, 3)
        def _(dw):
            cols = pl.ds(pl.multiple_of(dw * 256, 256), 256)
            both = halo[side].reshape(160, 256)
            p0 = jnp.dot(both, w[0, dh, cols], preferred_element_type=F32)
            p1 = jnp.dot(both[80:160], w[1, dh, cols], preferred_element_type=F32)
            nxt[0, dw, rows] += p0[0:80] + p1
            nxt[1, dw, rows] += p0[80:160]

        for f in range(2):
            zed_out[side, f] = joined(nxt, f, rows, 80).astype(BF16)

        @pl.when(has_next)
        def _():
            edge_copy(side).start()

        @pl.loop(0, 3)
        def _(dw):
            cols = pl.ds(pl.multiple_of(dw * 256, 256), 256)
            both = halo[side].reshape(160, 256)
            p0 = jnp.dot(both, w[2, dh, cols], preferred_element_type=F32)
            p1 = jnp.dot(both[0:80], w[1, dh, cols], preferred_element_type=F32)
            own[0, dw, rows] += p0[0:80]
            own[1, dw, rows] += p0[80:160] + p1

        for f in range(2):
            conv_edge[side, f] = joined(own, f, rows, 80)
        return carry

    lax.fori_loop(0, 2, side_step, 0)
    loads[4].wait()

    def finish(conv, base, target, first):
        size = conv.shape[0]
        mean = jnp.mean(conv * conv, axis=1, keepdims=True)
        v = conv * lax.rsqrt(mean + 1e-06) * gain_ref[...][None, :]
        out = (base.reshape(size, 256).astype(F32) + v / (1.0 + jnp.exp(-v))).astype(BF16)
        dims = (((0,), (0,)), ((), ()))
        g = lax.dot_general(out, out, dims, preferred_element_type=F32)
        c = lax.dot_general(out, target.reshape(size, 128), dims, preferred_element_type=F32)
        for i, block in enumerate((g[0:128, 0:128], g[0:128, 128:256], g[128:256, 128:256], c[0:128], c[128:256])):
            place = slice(128 * i, 128 * i + 128)
            pay[place] = block if first else pay[place] + block
        return out

    for f in range(2):
        @pl.when(has_prev)
        def _():
            inner_copy(f).wait_recv()

        conv = conv_in[f] + zin[f].reshape(320, 256).astype(F32)
        feat[f, 1:5] = finish(conv, win[f, 2:6], tgt[f, 1:5], f == 0).reshape(4, 80, 256)
    for side in range(2):
        @pl.when(has_prev)
        def _():
            edge_copy(side).wait_recv()

    conv = (conv_edge[...] + zed[...].astype(F32)).reshape(320, 256)
    base = jnp.concatenate([win[:, 1], win[:, 6]], axis=0)
    target = jnp.concatenate([tgt[:, 0], tgt[:, 5]], axis=0)
    out = finish(conv, base, target, False).reshape(2, 2, 80, 256)
    feat[:, 0] = out[0]
    feat[:, 5] = out[1]

    def copy(stage, me, peer, k, src, dst):
        j = (me + k) % 8
        return pltpu.make_async_remote_copy(
            src_ref=src(j), dst_ref=dst(me), send_sem=send_sem.at[stage, j], recv_sem=recv_sem.at[stage, me],
            device_id=peer(j), device_id_type=MESH,
        )

    def arrival(stage, me, peer, k, src, dst):
        j = (me + k) % 8
        return pltpu.make_async_remote_copy(
            src_ref=src(j), dst_ref=dst(j), send_sem=send_sem.at[stage, j], recv_sem=recv_sem.at[stage, j],
            device_id=peer(j), device_id_type=MESH,
        )

    def send(stage, me, peer, src, dst):
        for k in FAR:
            copy(stage, me, peer, k, src, dst).start()

    def receive(stage, me, peer, src, dst):
        for k in FAR:
            arrival(stage, me, peer, k, src, dst).wait_recv()

    def drain(stage, me, peer, src, dst):
        for k in FAR:
            copy(stage, me, peer, k, src, dst).wait_send()

    def chunk(ref):
        return lambda j: ref.at[pl.ds(pl.multiple_of(j * 80, 8), 80)]

    def slot(ref):
        return lambda j: ref.at[j]

    def total(ref):
        acc = ref[0].astype(F32)
        for j in range(1, 8):
            acc = acc + ref[j].astype(F32)
        return acc

    s0 = (0, a_me, a_peer, chunk(pay), slot(rs))
    send(*s0)
    rs[a_me] = pay[pl.ds(pl.multiple_of(a_me * 80, 8), 80)]
    receive(*s0)
    part = total(rs)
    ya[y_me] = part[0:48].astype(BF16)
    za[z_me] = part[48:80].astype(BF16)
    s1 = (1, y_me, y_peer, lambda j: ya.at[y_me], slot(ya))
    s2 = (2, z_me, z_peer, lambda j: za.at[z_me], slot(za))
    send(*s1)
    send(*s2)
    receive(*s1)
    zb[z_me] = total(ya).astype(BF16)
    s3 = (3, z_me, z_peer, lambda j: zb.at[z_me], slot(zb))
    send(*s3)
    receive(*s2)
    yb[y_me] = total(za).astype(BF16)
    s4 = (4, y_me, y_peer, lambda j: yb.at[y_me], slot(yb))
    send(*s4)
    receive(*s3)
    here = pl.multiple_of(a_me * 80, 8)
    fin[pl.ds(here, 48)] = total(zb)
    receive(*s4)
    fin[pl.ds(here + 48, 32)] = total(yb)
    s5 = (5, a_me, a_peer, lambda j: fin.at[pl.ds(here, 80)], chunk(fin))
    send(*s5)
    receive(*s5)

    for s in (s0, s1, s2, s3, s4, s5):
        drain(*s)

    @pl.when(has_down)
    def _():
        side_copy(0).wait_send()

    @pl.when(has_up)
    def _():
        side_copy(1).wait_send()

    @pl.when(has_next)
    def _():
        for i in range(2):
            inner_copy(i).wait_send()
            edge_copy(i).wait_send()


def write_kernel(scale, feat, fin, feat_out, gram_out, cross_out, gram, cross, sem):
    first = pltpu.make_async_copy(feat, feat_out, sem.at[0])
    first.start()
    cross[...] = fin[384:640] * scale
    second = pltpu.make_async_copy(cross, cross_out, sem.at[1])
    second.start()
    gram[0:128, 0:128] = fin[0:128] * scale
    gram[0:128, 128:256] = fin[128:256] * scale
    gram[128:256, 0:128] = fin[128:256].T * scale
    gram[128:256, 128:256] = fin[256:384] * scale
    third = pltpu.make_async_copy(gram, gram_out, sem.at[2])
    third.start()
    first.wait()
    second.wait()
    third.wait()


def on_device(latents, conv_weight, norm_gain, depth_target):
    vmem = pl.BlockSpec(memory_space=pltpu.VMEM)
    anywhere = pl.BlockSpec(memory_space=pltpu.HBM)
    dma = pltpu.SemaphoreType.DMA
    feat, fin = pl.pallas_call(
        layer_kernel,
        out_shape=(jax.ShapeDtypeStruct((2, 6, 80, 256), BF16), jax.ShapeDtypeStruct((640, 128), F32)),
        in_specs=[anywhere, anywhere, vmem, anywhere],
        out_specs=(vmem, vmem),
        scratch_shapes=[
            pltpu.VMEM((2, 8, 80, 256), BF16),
            pltpu.VMEM((3, 3, 768, 256), BF16),
            pltpu.VMEM((2, 6, 80, 128), BF16),
            pltpu.VMEM((2, 3, 480, 256), F32),
            pltpu.VMEM((2, 3, 480, 256), F32),
            pltpu.VMEM((2, 2, 80, 256), BF16),
            pltpu.VMEM((2, 320, 256), F32),
            pltpu.VMEM((2, 2, 80, 256), F32),
            pltpu.VMEM((2, 4, 80, 256), BF16),
            pltpu.VMEM((2, 4, 80, 256), BF16),
            pltpu.VMEM((2, 2, 80, 256), BF16),
            pltpu.VMEM((2, 2, 80, 256), BF16),
            pltpu.VMEM((640, 128), F32),
            pltpu.VMEM((8, 80, 128), F32),
            pltpu.VMEM((8, 48, 128), BF16),
            pltpu.VMEM((8, 32, 128), BF16),
            pltpu.VMEM((8, 32, 128), BF16),
            pltpu.VMEM((8, 48, 128), BF16),
            dma((5,)),
            dma((2,)),
            dma((2,)),
            dma((4,)),
            dma((4,)),
            dma((6, 8)),
            dma((6, 8)),
        ],
        compiler_params=pltpu.CompilerParams(collective_id=0, has_side_effects=True, vmem_limit_bytes=55_200_000),
    )(latents, conv_weight, norm_gain, depth_target)
    count = 960 * lax.axis_size("tm") * lax.axis_size("row")
    return pl.pallas_call(
        functools.partial(write_kernel, 1.0 / count),
        out_shape=(
            jax.ShapeDtypeStruct((2, 6, 80, 256), BF16),
            jax.ShapeDtypeStruct((256, 256), F32),
            jax.ShapeDtypeStruct((256, 128), F32),
        ),
        in_specs=[vmem, vmem],
        out_specs=(anywhere, anywhere, anywhere),
        scratch_shapes=[pltpu.VMEM((256, 256), F32), pltpu.VMEM((256, 128), F32), dma((3,))],
        compiler_params=pltpu.CompilerParams(vmem_limit_bytes=55_200_000),
    )(feat, fin)


def solution(mesh):
    in_specs = (P("tm", "row", None, None), P(), P(), P("tm", "row", None, None))
    out_specs = (P("tm", "row", None, None), P(), P())
    return jax.shard_map(
        on_device, mesh=mesh, in_specs=in_specs, out_specs=out_specs, check_vma=False
    )
```

time: 90.2 us -> 62.2 us (0.69)
  Pallas kernels: 35.2 us -> 59.8 us
  starting transfers between devices: 20.4 us -> 0 us
  waiting for transfers between devices: 17.2 us -> 0 us
  matrix products: 7.34 us -> 0 us
  local copies, waits for them, and re-layouts: 7.36 us -> 1.62 us
  other arithmetic: 1.49 us -> 0 us
    pallas_call x1 -> x2, Pallas kernels: 35.2 us -> 59.8 us  [the longest x1 58.8 us: on_device(): pl.pallas_call(layer_kernel, out_shape=(jax.ShapeDtypeStruct((2, 6, 80, 2...]
    ppermute x3 -> x0, starting transfers between devices: 20.4 us -> none  [the longest x1 13.5 us: extended(): lax.ppermute(tail, axis, [(i, (i + 1) % count) for i in range(ends)])]
    ppermute x3 -> x0, waiting for transfers between devices: 17.2 us -> none  [the longest x1 7.81 us: from_behind(): lax.ppermute(value, axis, [(source, source + steps) for source in range(f...]
    dot_general x11 -> x0, matrix products: 7.34 us -> none  [the longest x9 5.29 us: convolve(): jnp.dot(piece, conv_weight[dtime, drow], preferred_element_type=jnp.float32)]
    unnamed x13 -> x4, local copies, waits for them, and re-layouts: 4.13 us -> 1.62 us
    slice x3 -> x0, local copies, waits for them, and re-layouts: 2.17 us -> none  [the longest x1 1.25 us: convolve(): stacked[dtime:dtime + frames, drow:drow + rows]]
    concatenate x2 -> x0, other arithmetic: 1.08 us -> none  [the longest x1 0.75 us: extended(): jnp.concatenate([lax.ppermute(tail, axis, [(i, (i + 1) % count) for i in...]
    concatenate x1 -> x0, local copies, waits for them, and re-layouts: 1.07 us -> none  [on_device(): joined = jnp.concatenate([cached, latents], axis=0)]
  transfers between devices with their start and end apart: 3 -> 0, of which waited for: 3 -> 0; matrix products, arithmetic and copies ran while one was open for 0% -> 0% of each run, Pallas kernels for 0% -> 0%
where the time goes in v2:
time: 62.2 us; the launch traced here: 62 us
  Pallas kernels  59.8 us (96%)
  local copies, waits for them, and re-layouts  1.62 us (3%)
  between operations  0.65 us (1%)
    pallas_call x1, Pallas kernels, on_device(): pl.pallas_call(layer_kernel, out_shape=(jax.ShapeDtypeStruct((2, 6, 80, 2...  58.8 us
    unnamed x4, local copies, waits for them, and re-layouts  1.62 us

profile of v2, /device:TPU:1, one launch (start us, length us, event | category | flops | bytes accessed | tf_op | source)
XLA Modules:
  0.0 62.0 jit_solution(15578551585773796397)
XLA Ops:
  0.6 0.0 copy-start
  0.6 0.9 %copy-done = bf16[2,6,80,128]{3,2,1,0:T(8,128)(2,1)S(1)} copy-done((bf16[2,6,80,128]{3,2,1,0:T(8,128)(2,1)S(1)}, bf16[2,6,80,128]{3,2,1,0:T(8,128)(2,1)}, u32[]{:S(2)}) %copy-start) | copy-done | bytes 245784
  1.6 0.0 copy-start.1
  1.6 0.7 %copy-done.1 = f32[256]{0:T(256)S(1)} copy-done((f32[256]{0:T(256)S(1)}, f32[256]{0:T(256)}, u32[]{:S(2)}) %copy-start.1) | copy-done | bytes 1048
  2.3 58.8 %shard_map.67 = (bf16[2,6,80,256]{3,2,1,0:T(8,128)(2,1)S(1)}, f32[640,128]{1,0:T(8,128)S(1)}) custom-call(bf16[2,6,80,256]{3,2,1,0:T(8,128)(2,1)} %lat_hbm.1, bf16[3,3,768,256]{3,2,1,0:T(8,128)(2,1)} %w_hbm.1, f32[256]{0:T(256)S(1)} %copy-done.1, bf16[2,6,80,128]{3,2,1,0:T(8,128)(2,1)S(1)} %copy-done), custom_call_target="tpu_custom_call" | custom-call | tf_op jit(solution)/shard_map/pallas_call | solution.py:315
  61.1 0.9 %shard_map.68 = (bf16[2,6,80,256]{3,2,1,0:T(8,128)(2,1)}, f32[256,256]{1,0:T(8,128)}, f32[256,128]{1,0:T(8,128)}) custom-call(bf16[2,6,80,256]{3,2,1,0:T(8,128)(2,1)S(1)} %get-tuple-element.5.feat, f32[640,128]{1,0:T(8,128)S(1)} %get-tuple-element.6.fin), custom_call_target="tpu_custom_call" | custom-call | tf_op jit(solution)/shard_map/pallas_call | solution.py:350
Async XLA Ops:
  0.6 0.9 %copy-start = (bf16[2,6,80,128]{3,2,1,0:T(8,128)(2,1)S(1)}, bf16[2,6,80,128]{3,2,1,0:T(8,128)(2,1)}, u32[]{:S(2)}) copy-start(bf16[2,6,80,128]{3,2,1,0:T(8,128)(2,1)} %tgt_hbm.1) | copy-start | bytes 737284
  1.6 0.7 %copy-start.1 = (f32[256]{0:T(256)S(1)}, f32[256]{0:T(256)}, u32[]{:S(2)}) copy-start(f32[256]{0:T(256)} %gain_ref.1) | copy-start | bytes 3076

commit v3 on v2

--- a/solution.py
+++ b/solution.py
@@ -15,9 +15,9 @@
 
 
 def layer_kernel(
-    lat_hbm, w_hbm, gain_ref, tgt_hbm, feat, fin,
-    win, w, tgt, own, nxt, halo, conv_in, conv_edge, zin_out, zin, zed_out, zed,
-    pay, rs, ya, za, yb, zb, load_sem, side_send, side_recv, z_send, z_recv, send_sem, recv_sem,
+    lat_hbm, w_hbm, gain_hbm, tgt_hbm, feat, fin,
+    win, w, tgt, gain_ref, own, nxt, halo, conv_in, conv_edge, zin_out, zin, zed_out, zed,
+    sums, gpay, grs, crs, ya, za, yb, zb, load_sem, side_send, side_recv, z_send, z_recv, send_sem, recv_sem,
 ):
     tm = lax.axis_index("tm")
     row = lax.axis_index("row")
@@ -51,6 +51,7 @@
     loads = [pltpu.make_async_copy(lat_hbm, win.at[:, 1:7], load_sem.at[0])]
     loads += [pltpu.make_async_copy(w_hbm.at[dt], w.at[dt], load_sem.at[1 + dt]) for dt in range(3)]
     loads += [pltpu.make_async_copy(tgt_hbm, tgt, load_sem.at[4])]
+    loads += [pltpu.make_async_copy(gain_hbm, gain_ref, load_sem.at[5])]
     for load in loads:
         load.start()
     blank = jnp.zeros((2, 80, 256), BF16)
@@ -70,18 +71,17 @@
         zin[...] = jnp.zeros(zin.shape, BF16)
         zed[...] = jnp.zeros(zed.shape, BF16)
 
-    def taps(dst, outs):
+    def taps(dst, o, pairs):
         @pl.loop(0, 3)
         def _(dw):
             cols = pl.ds(pl.multiple_of(dw * 256, 256), 256)
-            for o, pairs in enumerate(outs):
-                acc = None
-                for frame, dt in pairs:
-                    for dh in range(3):
-                        piece = win[frame, dh : dh + 6].reshape(480, 256)
-                        prod = jnp.dot(piece, w[dt, dh, cols], preferred_element_type=F32)
-                        acc = prod if acc is None else acc + prod
-                dst[o, dw] = acc
+            acc = None
+            for frame, dt in pairs:
+                for dh in range(3):
+                    piece = win[frame, dh : dh + 6].reshape(480, 256)
+                    prod = jnp.dot(piece, w[dt, dh, cols], preferred_element_type=F32)
+                    acc = prod if acc is None else acc + prod
+            dst[o, dw] = acc
 
     def joined(src, o, rows, size):
         col = lax.broadcasted_iota(jnp.int32, (size, 1), 0) % 80
@@ -89,10 +89,10 @@
         right = jnp.where(col == 79, 0.0, pltpu.roll(src[o, 2, rows], size - 1, 0))
         return src[o, 1, rows] + left + right
 
-    for load in loads[:3]:
-        load.wait()
-    taps(nxt, NEXT)
-    for f in range(2):
+    loads[0].wait()
+    for f in (1, 0):
+        loads[2 - f].wait()
+        taps(nxt, f, NEXT[f])
         zin_out[f] = joined(nxt, f, pl.ds(80, 320), 320).astype(BF16).reshape(4, 80, 256)
     pl.semaphore_wait(barrier, expected)
 
@@ -124,12 +124,12 @@
 
     @pl.when(has_next)
     def _():
+        inner_copy(1).start()
         inner_copy(0).start()
-        inner_copy(1).start()
 
     loads[3].wait()
-    taps(own, OWN)
     for f in range(2):
+        taps(own, f, OWN[f])
         conv_in[f] = joined(own, f, pl.ds(80, 320), 320)
 
     def side_step(i, carry):
@@ -174,6 +174,7 @@
 
     lax.fori_loop(0, 2, side_step, 0)
     loads[4].wait()
+    loads[5].wait()
 
     def finish(conv, base, target, first):
         size = conv.shape[0]
@@ -183,18 +184,19 @@
         dims = (((0,), (0,)), ((), ()))
         g = lax.dot_general(out, out, dims, preferred_element_type=F32)
         c = lax.dot_general(out, target.reshape(size, 128), dims, preferred_element_type=F32)
-        for i, block in enumerate((g[0:128, 0:128], g[0:128, 128:256], g[128:256, 128:256], c[0:128], c[128:256])):
+        blocks = (g[0:128, 0:128], g[0:128, 128:256], g[128:256, 128:256], c[0:128], c[128:256])
+        for i, block in enumerate(blocks):
             place = slice(128 * i, 128 * i + 128)
-            pay[place] = block if first else pay[place] + block
+            sums[place] = block if first else sums[place] + block
         return out
 
-    for f in range(2):
+    for f in (1, 0):
         @pl.when(has_prev)
         def _():
             inner_copy(f).wait_recv()
 
         conv = conv_in[f] + zin[f].reshape(320, 256).astype(F32)
-        feat[f, 1:5] = finish(conv, win[f, 2:6], tgt[f, 1:5], f == 0).reshape(4, 80, 256)
+        feat[f, 1:5] = finish(conv, win[f, 2:6], tgt[f, 1:5], f == 1).reshape(4, 80, 256)
     for side in range(2):
         @pl.when(has_prev)
         def _():
@@ -233,8 +235,8 @@
         for k in FAR:
             copy(stage, me, peer, k, src, dst).wait_send()
 
-    def chunk(ref):
-        return lambda j: ref.at[pl.ds(pl.multiple_of(j * 80, 8), 80)]
+    def chunk(ref, size):
+        return lambda j: ref.at[pl.ds(pl.multiple_of(j * size, 8), size)]
 
     def slot(ref):
         return lambda j: ref.at[j]
@@ -245,35 +247,43 @@
             acc = acc + ref[j].astype(F32)
         return acc
 
-    s0 = (0, a_me, a_peer, chunk(pay), slot(rs))
+    gpay[...] = sums[0:384].astype(BF16)
+    gplace = pl.ds(pl.multiple_of(a_me * 48, 16), 48)
+    cplace = pl.ds(pl.multiple_of(384 + a_me * 32, 8), 32)
+    s0 = (0, a_me, a_peer, chunk(gpay, 48), slot(grs))
+    s1 = (1, a_me, a_peer, lambda j: sums.at[pl.ds(pl.multiple_of(384 + j * 32, 8), 32)], slot(crs))
     send(*s0)
-    rs[a_me] = pay[pl.ds(pl.multiple_of(a_me * 80, 8), 80)]
+    send(*s1)
+    grs[a_me] = gpay[gplace]
+    crs[a_me] = sums[cplace]
     receive(*s0)
-    part = total(rs)
-    ya[y_me] = part[0:48].astype(BF16)
-    za[z_me] = part[48:80].astype(BF16)
-    s1 = (1, y_me, y_peer, lambda j: ya.at[y_me], slot(ya))
-    s2 = (2, z_me, z_peer, lambda j: za.at[z_me], slot(za))
-    send(*s1)
+    ya[y_me] = total(grs).astype(BF16)
+    s2 = (2, y_me, y_peer, lambda j: ya.at[y_me], slot(ya))
     send(*s2)
     receive(*s1)
-    zb[z_me] = total(ya).astype(BF16)
-    s3 = (3, z_me, z_peer, lambda j: zb.at[z_me], slot(zb))
+    za[z_me] = total(crs)
+    s3 = (3, z_me, z_peer, lambda j: za.at[z_me], slot(za))
     send(*s3)
     receive(*s2)
-    yb[y_me] = total(za).astype(BF16)
-    s4 = (4, y_me, y_peer, lambda j: yb.at[y_me], slot(yb))
+    zb[z_me] = total(ya).astype(BF16)
+    s4 = (4, z_me, z_peer, lambda j: zb.at[z_me], slot(zb))
     send(*s4)
     receive(*s3)
-    here = pl.multiple_of(a_me * 80, 8)
-    fin[pl.ds(here, 48)] = total(zb)
+    yb[y_me] = total(za)
+    s5 = (5, y_me, y_peer, lambda j: yb.at[y_me], slot(yb))
+    send(*s5)
     receive(*s4)
-    fin[pl.ds(here + 48, 32)] = total(yb)
-    s5 = (5, a_me, a_peer, lambda j: fin.at[pl.ds(here, 80)], chunk(fin))
-    send(*s5)
+    fin[pl.ds(pl.multiple_of(a_me * 48, 16), 48)] = total(zb)
+    s6 = (6, a_me, a_peer, lambda j: fin.at[gplace], chunk(fin, 48))
+    send(*s6)
     receive(*s5)
-
-    for s in (s0, s1, s2, s3, s4, s5):
+    fin[cplace] = total(yb)
+    s7 = (7, a_me, a_peer, lambda j: fin.at[cplace], lambda j: fin.at[pl.ds(pl.multiple_of(384 + j * 32, 8), 32)])
+    send(*s7)
+    receive(*s6)
+    receive(*s7)
+
+    for s in (s0, s1, s2, s3, s4, s5, s6, s7):
         drain(*s)
 
     @pl.when(has_down)
@@ -315,12 +325,13 @@
     feat, fin = pl.pallas_call(
         layer_kernel,
         out_shape=(jax.ShapeDtypeStruct((2, 6, 80, 256), BF16), jax.ShapeDtypeStruct((640, 128), F32)),
-        in_specs=[anywhere, anywhere, vmem, anywhere],
+        in_specs=[anywhere, anywhere, anywhere, anywhere],
         out_specs=(vmem, vmem),
         scratch_shapes=[
             pltpu.VMEM((2, 8, 80, 256), BF16),
             pltpu.VMEM((3, 3, 768, 256), BF16),
             pltpu.VMEM((2, 6, 80, 128), BF16),
+            pltpu.VMEM((256,), F32),
             pltpu.VMEM((2, 3, 480, 256), F32),
             pltpu.VMEM((2, 3, 480, 256), F32),
             pltpu.VMEM((2, 2, 80, 256), BF16),
@@ -331,21 +342,23 @@
             pltpu.VMEM((2, 2, 80, 256), BF16),
             pltpu.VMEM((2, 2, 80, 256), BF16),
             pltpu.VMEM((640, 128), F32),
-            pltpu.VMEM((8, 80, 128), F32),
+            pltpu.VMEM((384, 128), BF16),
             pltpu.VMEM((8, 48, 128), BF16),
-            pltpu.VMEM((8, 32, 128), BF16),
-            pltpu.VMEM((8, 32, 128), BF16),
+            pltpu.VMEM((8, 32, 128), F32),
             pltpu.VMEM((8, 48, 128), BF16),
-            dma((5,)),
+            pltpu.VMEM((8, 32, 128), F32),
+            pltpu.VMEM((8, 32, 128), F32),
+            pltpu.VMEM((8, 48, 128), BF16),
+            dma((6,)),
             dma((2,)),
             dma((2,)),
             dma((4,)),
             dma((4,)),
-            dma((6, 8)),
-            dma((6, 8)),
+            dma((8, 8)),
+            dma((8, 8)),
         ],
-        compiler_params=pltpu.CompilerParams(collective_id=0, has_side_effects=True, vmem_limit_bytes=55_200_000),
-    )(latents, conv_weight, norm_gain, depth_target)
+        compiler_params=pltpu.CompilerParams(collective_id=0, has_side_effects=True, vmem_limit_bytes=40 << 20),
+    )(*(pltpu.with_memory_space_constraint(a, pltpu.HBM) for a in (latents, conv_weight, norm_gain, depth_target)))
     count = 960 * lax.axis_size("tm") * lax.axis_size("row")
     return pl.pallas_call(
         functools.partial(write_kernel, 1.0 / count),
@@ -357,7 +370,7 @@
         in_specs=[vmem, vmem],
         out_specs=(anywhere, anywhere, anywhere),
         scratch_shapes=[pltpu.VMEM((256, 256), F32), pltpu.VMEM((256, 128), F32), dma((3,))],
-        compiler_params=pltpu.CompilerParams(vmem_limit_bytes=55_200_000),
+        compiler_params=pltpu.CompilerParams(vmem_limit_bytes=40 << 20),
     )(feat, fin)
 
 

time: 62.2 us -> 59.8 us (0.961)
  local copies, waits for them, and re-layouts: 1.62 us -> 0 us
  Pallas kernels: 59.8 us -> 59.1 us
    unnamed x4 -> x0, local copies, waits for them, and re-layouts: 1.62 us -> none
    pallas_call x1, Pallas kernels: 58.8 us -> 58.1 us  [on_device(): pl.pallas_call(layer_kernel, out_shape=(jax.ShapeDtypeStruct((2, 6, 80, 2...]
where the time goes in v3:
time: 59.8 us; the launch traced here: 59.7 us
  Pallas kernels  59.1 us (99%)
  between operations  0.64 us (1%)
    pallas_call x1, Pallas kernels, on_device(): pl.pallas_call(layer_kernel, out_shape=(jax.ShapeDtypeStruct((2, 6, 80, 2...  58.1 us

profile of v3, /device:TPU:1, one launch (start us, length us, event | category | flops | bytes accessed | tf_op | source)
XLA Modules:
  0.0 59.7 jit_solution(15917741756208089520)
XLA Ops:
  0.6 58.1 %shard_map.67 = (bf16[2,6,80,256]{3,2,1,0:T(8,128)(2,1)S(1)}, f32[640,128]{1,0:T(8,128)S(1)}) custom-call(bf16[2,6,80,256]{3,2,1,0:T(8,128)(2,1)} %lat_hbm.1, bf16[3,3,768,256]{3,2,1,0:T(8,128)(2,1)} %w_hbm.1, f32[256]{0:T(256)} %gain_hbm.1, bf16[2,6,80,128]{3,2,1,0:T(8,128)(2,1)} %tgt_hbm.1), custom_call_target="tpu_custom_call" | custom-call | tf_op jit(solution)/shard_map/pallas_call | solution.py:325
  58.8 0.9 %shard_map.68 = (bf16[2,6,80,256]{3,2,1,0:T(8,128)(2,1)}, f32[256,256]{1,0:T(8,128)}, f32[256,128]{1,0:T(8,128)}) custom-call(bf16[2,6,80,256]{3,2,1,0:T(8,128)(2,1)S(1)} %get-tuple-element.5.feat, f32[640,128]{1,0:T(8,128)S(1)} %get-tuple-element.6.fin), custom_call_target="tpu_custom_call" | custom-call | tf_op jit(solution)/shard_map/pallas_call | solution.py:363

commit v4 on v3

--- a/solution.py
+++ b/solution.py
@@ -90,50 +90,47 @@
         return src[o, 1, rows] + left + right
 
     loads[0].wait()
+    pl.semaphore_wait(barrier, expected)
+
+    def side_copy(to):
+        return pltpu.make_async_remote_copy(
+            src_ref=win.at[:, 6 - 5 * to], dst_ref=halo.at[to], send_sem=side_send.at[to], recv_sem=side_recv.at[to],
+            device_id=(tm, row + 1 - 2 * to), device_id_type=MESH,
+        )
+
+    def inner_copy(f):
+        return pltpu.make_async_remote_copy(
+            src_ref=zin_out.at[f], dst_ref=zin.at[f], send_sem=z_send.at[f], recv_sem=z_recv.at[f],
+            device_id=(tm + 1, row), device_id_type=MESH,
+        )
+
+    def edge_copy(side):
+        return pltpu.make_async_remote_copy(
+            src_ref=zed_out.at[side], dst_ref=zed.at[side], send_sem=z_send.at[2 + side], recv_sem=z_recv.at[2 + side],
+            device_id=(tm + 1, row), device_id_type=MESH,
+        )
+
+    @pl.when(has_down)
+    def _():
+        side_copy(0).start()
+
+    @pl.when(has_up)
+    def _():
+        side_copy(1).start()
+
     for f in (1, 0):
         loads[2 - f].wait()
         taps(nxt, f, NEXT[f])
         zin_out[f] = joined(nxt, f, pl.ds(80, 320), 320).astype(BF16).reshape(4, 80, 256)
-    pl.semaphore_wait(barrier, expected)
-
-    def side_copy(to):
-        return pltpu.make_async_remote_copy(
-            src_ref=win.at[:, 6 - 5 * to], dst_ref=halo.at[to], send_sem=side_send.at[to], recv_sem=side_recv.at[to],
-            device_id=(tm, row + 1 - 2 * to), device_id_type=MESH,
-        )
-
-    def inner_copy(f):
-        return pltpu.make_async_remote_copy(
-            src_ref=zin_out.at[f], dst_ref=zin.at[f], send_sem=z_send.at[f], recv_sem=z_recv.at[f],
-            device_id=(tm + 1, row), device_id_type=MESH,
-        )
-
-    def edge_copy(side):
-        return pltpu.make_async_remote_copy(
-            src_ref=zed_out.at[side], dst_ref=zed.at[side], send_sem=z_send.at[2 + side], recv_sem=z_recv.at[2 + side],
-            device_id=(tm + 1, row), device_id_type=MESH,
-        )
-
-    @pl.when(has_down)
-    def _():
-        side_copy(0).start()
-
-    @pl.when(has_up)
-    def _():
-        side_copy(1).start()
-
-    @pl.when(has_next)
-    def _():
-        inner_copy(1).start()
-        inner_copy(0).start()
-
-    loads[3].wait()
-    for f in range(2):
-        taps(own, f, OWN[f])
-        conv_in[f] = joined(own, f, pl.ds(80, 320), 320)
-
-    def side_step(i, carry):
-        side = (1 - core) * (1 - i) + core * i
+
+        @pl.when(has_next)
+        def _():
+            inner_copy(f).start()
+
+    def edge_rows(side):
+        return pl.ds(pl.multiple_of(side * 400, 80), 80)
+
+    def edge_next(side):
         other = row + 2 * side - 1
 
         @pl.when((other >= 0) & (other <= 15))
@@ -141,7 +138,7 @@
             side_copy(side).wait_recv()
 
         dh = 2 * side
-        rows = pl.ds(pl.multiple_of(side * 400, 80), 80)
+        rows = edge_rows(side)
 
         @pl.loop(0, 3)
         def _(dw):
@@ -159,6 +156,19 @@
         def _():
             edge_copy(side).start()
 
+    near_side, far_side = 1 - core, core
+    edge_next(near_side)
+
+    loads[3].wait()
+    for f in range(2):
+        taps(own, f, OWN[f])
+        conv_in[f] = joined(own, f, pl.ds(80, 320), 320)
+    edge_next(far_side)
+
+    def edge_own(side, carry):
+        dh = 2 * side
+        rows = edge_rows(side)
+
         @pl.loop(0, 3)
         def _(dw):
             cols = pl.ds(pl.multiple_of(dw * 256, 256), 256)
@@ -172,7 +182,7 @@
             conv_edge[side, f] = joined(own, f, rows, 80)
         return carry
 
-    lax.fori_loop(0, 2, side_step, 0)
+    lax.fori_loop(0, 2, edge_own, 0)
     loads[4].wait()
     loads[5].wait()
 
@@ -197,17 +207,14 @@
 
         conv = conv_in[f] + zin[f].reshape(320, 256).astype(F32)
         feat[f, 1:5] = finish(conv, win[f, 2:6], tgt[f, 1:5], f == 1).reshape(4, 80, 256)
-    for side in range(2):
+    for side in (near_side, far_side):
         @pl.when(has_prev)
         def _():
             edge_copy(side).wait_recv()
 
-    conv = (conv_edge[...] + zed[...].astype(F32)).reshape(320, 256)
-    base = jnp.concatenate([win[:, 1], win[:, 6]], axis=0)
-    target = jnp.concatenate([tgt[:, 0], tgt[:, 5]], axis=0)
-    out = finish(conv, base, target, False).reshape(2, 2, 80, 256)
-    feat[:, 0] = out[0]
-    feat[:, 5] = out[1]
+        conv = (conv_edge[side] + zed[side].astype(F32)).reshape(160, 256)
+        out = finish(conv, win[:, 1 + 5 * side], tgt[:, 5 * side], False)
+        feat[:, 5 * side] = out.reshape(2, 80, 256)
 
     def copy(stage, me, peer, k, src, dst):
         j = (me + k) % 8

time: 59.8 us -> 59.7 us (level)
  no operation moved by 1% of the time
where the time goes in v4:
time: 59.7 us; the launch traced here: 59.6 us
  Pallas kernels  58.9 us (99%)
  between operations  0.64 us (1%)
    pallas_call x1, Pallas kernels, on_device(): pl.pallas_call(layer_kernel, out_shape=(jax.ShapeDtypeStruct((2, 6, 80, 2...  58 us

profile of v4, /device:TPU:1, one launch (start us, length us, event | category | flops | bytes accessed | tf_op | source)
XLA Modules:
  0.0 59.6 jit_solution(3549422590168289490)
XLA Ops:
  0.6 58.0 %shard_map.67 = (bf16[2,6,80,256]{3,2,1,0:T(8,128)(2,1)S(1)}, f32[640,128]{1,0:T(8,128)S(1)}) custom-call(bf16[2,6,80,256]{3,2,1,0:T(8,128)(2,1)} %lat_hbm.1, bf16[3,3,768,256]{3,2,1,0:T(8,128)(2,1)} %w_hbm.1, f32[256]{0:T(256)} %gain_hbm.1, bf16[2,6,80,128]{3,2,1,0:T(8,128)(2,1)} %tgt_hbm.1), custom_call_target="tpu_custom_call" | custom-call | tf_op jit(solution)/shard_map/pallas_call | solution.py:332
  58.6 0.9 %shard_map.68 = (bf16[2,6,80,256]{3,2,1,0:T(8,128)(2,1)}, f32[256,256]{1,0:T(8,128)}, f32[256,128]{1,0:T(8,128)}) custom-call(bf16[2,6,80,256]{3,2,1,0:T(8,128)(2,1)S(1)} %get-tuple-element.5.feat, f32[640,128]{1,0:T(8,128)S(1)} %get-tuple-element.6.fin), custom_call_target="tpu_custom_call" | custom-call | tf_op jit(solution)/shard_map/pallas_call | solution.py:370

commit v5 on v4

--- a/solution.py
+++ b/solution.py
@@ -16,8 +16,8 @@
 
 def layer_kernel(
     lat_hbm, w_hbm, gain_hbm, tgt_hbm, feat, fin,
-    win, w, tgt, gain_ref, own, nxt, halo, conv_in, conv_edge, zin_out, zin, zed_out, zed,
-    sums, gpay, grs, crs, ya, za, yb, zb, load_sem, side_send, side_recv, z_send, z_recv, send_sem, recv_sem,
+    win, w, tgt, gain_ref, own, nxt, halo, passing, conv_in, conv_edge, zin_out, zin, zed_out, zed,
+    sums, gpay, grs, crs, ya, za, yb, zb, load_sem, side_send, side_recv, relay_sem, z_send, z_recv, send_sem, recv_sem,
 ):
     tm = lax.axis_index("tm")
     row = lax.axis_index("row")
@@ -36,6 +36,16 @@
     a_me, y_me, z_me = x * 2 + core, y, zh * 4 + zl
     has_prev, has_next, has_up, has_down = tm > 0, tm < 31, row > 0, row < 15
 
+    z = zh * 4 + zl
+
+    def ring(zz, xx):
+        return y * 4 + zz % 4, xx * 4 + (zz // 4) * 2
+
+    relay = ring((z + 6) % 8, x)
+    origin_tm, origin_row = ring((z + 2) % 8, x)
+    relays = (core == 0) & (origin_row > 0)
+    relayed_by = ring(((((row + 1) // 2) % 2) * 4 + zl + 6) % 8, (row + 1) // 4)
+
     barrier = pltpu.get_barrier_semaphore()
     near = ((has_prev, (tm - 1, row)), (has_next, (tm + 1, row)), (has_up, (tm, row - 1)), (has_down, (tm, row + 1)))
     expected = jnp.int32(21)
@@ -44,6 +54,11 @@
         def _():
             pl.semaphore_signal(barrier, inc=1, device_id=device, device_id_type=MESH)
         expected = expected + there.astype(jnp.int32)
+    @pl.when((core == 1) & has_down)
+    def _():
+        pl.semaphore_signal(barrier, inc=1, device_id=relayed_by, device_id_type=MESH)
+
+    expected = expected + relays.astype(jnp.int32)
     for me, peer in ((a_me, a_peer), (y_me, y_peer), (z_me, z_peer)):
         for k in range(1, 8):
             pl.semaphore_signal(barrier, inc=1, device_id=peer((me + k) % 8), device_id_type=MESH)
@@ -114,7 +129,23 @@
     def _():
         side_copy(0).start()
 
-    @pl.when(has_up)
+    def relay_in():
+        return pltpu.make_async_remote_copy(
+            src_ref=win.at[:, 1], dst_ref=passing, send_sem=side_send.at[1], recv_sem=relay_sem.at[0],
+            device_id=relay, device_id_type=MESH,
+        )
+
+    def relay_out():
+        return pltpu.make_async_remote_copy(
+            src_ref=passing, dst_ref=halo.at[1], send_sem=relay_sem.at[1], recv_sem=side_recv.at[1],
+            device_id=(origin_tm, origin_row - 1), device_id_type=MESH,
+        )
+
+    @pl.when((core == 0) & has_up)
+    def _():
+        relay_in().start()
+
+    @pl.when(core == 1)
     def _():
         side_copy(1).start()
 
@@ -158,6 +189,11 @@
 
     near_side, far_side = 1 - core, core
     edge_next(near_side)
+
+    @pl.when(relays)
+    def _():
+        relay_in().wait_recv()
+        relay_out().start()
 
     loads[3].wait()
     for f in range(2):
@@ -301,6 +337,10 @@
     def _():
         side_copy(1).wait_send()
 
+    @pl.when(relays)
+    def _():
+        relay_out().wait_send()
+
     @pl.when(has_next)
     def _():
         for i in range(2):
@@ -342,6 +382,7 @@
             pltpu.VMEM((2, 3, 480, 256), F32),
             pltpu.VMEM((2, 3, 480, 256), F32),
             pltpu.VMEM((2, 2, 80, 256), BF16),
+            pltpu.VMEM((2, 80, 256), BF16),
             pltpu.VMEM((2, 320, 256), F32),
             pltpu.VMEM((2, 2, 80, 256), F32),
             pltpu.VMEM((2, 4, 80, 256), BF16),
@@ -357,6 +398,7 @@
             pltpu.VMEM((8, 32, 128), F32),
             pltpu.VMEM((8, 48, 128), BF16),
             dma((6,)),
+            dma((2,)),
             dma((2,)),
             dma((2,)),
             dma((4,)),

time: 59.7 us -> 61.8 us (1.035)
  Pallas kernels: 58.9 us -> 61 us
    pallas_call x1, Pallas kernels: 58 us -> 60.1 us  [on_device(): pl.pallas_call(layer_kernel, out_shape=(jax.ShapeDtypeStruct((2, 6, 80, 2...]
where the time goes in v5:
time: 61.8 us; the launch traced here: 61.7 us
  Pallas kernels  61 us (99%)
  between operations  0.64 us (1%)
    pallas_call x1, Pallas kernels, on_device(): pl.pallas_call(layer_kernel, out_shape=(jax.ShapeDtypeStruct((2, 6, 80, 2...  60.1 us

profile of v5, /device:TPU:1, one launch (start us, length us, event | category | flops | bytes accessed | tf_op | source)
XLA Modules:
  0.0 61.7 jit_solution(12647137532786602894)
XLA Ops:
  0.6 60.1 %shard_map.67 = (bf16[2,6,80,256]{3,2,1,0:T(8,128)(2,1)S(1)}, f32[640,128]{1,0:T(8,128)S(1)}) custom-call(bf16[2,6,80,256]{3,2,1,0:T(8,128)(2,1)} %lat_hbm.1, bf16[3,3,768,256]{3,2,1,0:T(8,128)(2,1)} %w_hbm.1, f32[256]{0:T(256)} %gain_hbm.1, bf16[2,6,80,128]{3,2,1,0:T(8,128)(2,1)} %tgt_hbm.1), custom_call_target="tpu_custom_call" | custom-call | tf_op jit(solution)/shard_map/pallas_call | solution.py:372
  60.7 0.9 %shard_map.68 = (bf16[2,6,80,256]{3,2,1,0:T(8,128)(2,1)}, f32[256,256]{1,0:T(8,128)}, f32[256,128]{1,0:T(8,128)}) custom-call(bf16[2,6,80,256]{3,2,1,0:T(8,128)(2,1)S(1)} %get-tuple-element.5.feat, f32[640,128]{1,0:T(8,128)S(1)} %get-tuple-element.6.fin), custom_call_target="tpu_custom_call" | custom-call | tf_op jit(solution)/shard_map/pallas_call | solution.py:412

commit v6 on v4

--- a/solution.py
+++ b/solution.py
@@ -52,8 +52,8 @@
     loads += [pltpu.make_async_copy(w_hbm.at[dt], w.at[dt], load_sem.at[1 + dt]) for dt in range(3)]
     loads += [pltpu.make_async_copy(tgt_hbm, tgt, load_sem.at[4])]
     loads += [pltpu.make_async_copy(gain_hbm, gain_ref, load_sem.at[5])]
-    for load in loads:
-        load.start()
+    for i in (0, 3, 2, 1, 4, 5):
+        loads[i].start()
     blank = jnp.zeros((2, 80, 256), BF16)
     win[:, 0] = blank
     win[:, 7] = blank
@@ -118,8 +118,12 @@
     def _():
         side_copy(1).start()
 
+    for f in range(2):
+        loads[3 - f].wait()
+        taps(own, f, OWN[f])
+        conv_in[f] = joined(own, f, pl.ds(80, 320), 320)
+    loads[1].wait()
     for f in (1, 0):
-        loads[2 - f].wait()
         taps(nxt, f, NEXT[f])
         zin_out[f] = joined(nxt, f, pl.ds(80, 320), 320).astype(BF16).reshape(4, 80, 256)
 
@@ -159,10 +163,6 @@
     near_side, far_side = 1 - core, core
     edge_next(near_side)
 
-    loads[3].wait()
-    for f in range(2):
-        taps(own, f, OWN[f])
-        conv_in[f] = joined(own, f, pl.ds(80, 320), 320)
     edge_next(far_side)
 
     def edge_own(side, carry):

time: 59.7 us -> 54.8 us (0.918)
  Pallas kernels: 58.9 us -> 54.1 us
    pallas_call x1, Pallas kernels: 58 us -> 53.1 us  [on_device(): pl.pallas_call(layer_kernel, out_shape=(jax.ShapeDtypeStruct((2, 6, 80, 2...]
where the time goes in v6:
time: 54.8 us; the launch traced here: 54.7 us
  Pallas kernels  54.1 us (99%)
  between operations  0.64 us (1%)
    pallas_call x1, Pallas kernels, on_device(): pl.pallas_call(layer_kernel, out_shape=(jax.ShapeDtypeStruct((2, 6, 80, 2...  53.1 us

profile of v6, /device:TPU:1, one launch (start us, length us, event | category | flops | bytes accessed | tf_op | source)
XLA Modules:
  0.0 54.7 jit_solution(8965580428682771763)
XLA Ops:
  0.6 53.1 %shard_map.67 = (bf16[2,6,80,256]{3,2,1,0:T(8,128)(2,1)S(1)}, f32[640,128]{1,0:T(8,128)S(1)}) custom-call(bf16[2,6,80,256]{3,2,1,0:T(8,128)(2,1)} %lat_hbm.1, bf16[3,3,768,256]{3,2,1,0:T(8,128)(2,1)} %w_hbm.1, f32[256]{0:T(256)} %gain_hbm.1, bf16[2,6,80,128]{3,2,1,0:T(8,128)(2,1)} %tgt_hbm.1), custom_call_target="tpu_custom_call" | custom-call | tf_op jit(solution)/shard_map/pallas_call | solution.py:332
  53.8 0.9 %shard_map.68 = (bf16[2,6,80,256]{3,2,1,0:T(8,128)(2,1)}, f32[256,256]{1,0:T(8,128)}, f32[256,128]{1,0:T(8,128)}) custom-call(bf16[2,6,80,256]{3,2,1,0:T(8,128)(2,1)S(1)} %get-tuple-element.5.feat, f32[640,128]{1,0:T(8,128)S(1)} %get-tuple-element.6.fin), custom_call_target="tpu_custom_call" | custom-call | tf_op jit(solution)/shard_map/pallas_call | solution.py:370

commit v7 on v6

--- a/solution.py
+++ b/solution.py
@@ -38,15 +38,15 @@
 
     barrier = pltpu.get_barrier_semaphore()
     near = ((has_prev, (tm - 1, row)), (has_next, (tm + 1, row)), (has_up, (tm, row - 1)), (has_down, (tm, row + 1)))
+    for k in FAR:
+        for me, peer in ((z_me, z_peer), (y_me, y_peer), (a_me, a_peer)):
+            pl.semaphore_signal(barrier, inc=1, device_id=peer((me + k) % 8), device_id_type=MESH)
     expected = jnp.int32(21)
     for there, device in near:
         @pl.when(there)
         def _():
             pl.semaphore_signal(barrier, inc=1, device_id=device, device_id_type=MESH)
         expected = expected + there.astype(jnp.int32)
-    for me, peer in ((a_me, a_peer), (y_me, y_peer), (z_me, z_peer)):
-        for k in range(1, 8):
-            pl.semaphore_signal(barrier, inc=1, device_id=peer((me + k) % 8), device_id_type=MESH)
 
     loads = [pltpu.make_async_copy(lat_hbm, win.at[:, 1:7], load_sem.at[0])]
     loads += [pltpu.make_async_copy(w_hbm.at[dt], w.at[dt], load_sem.at[1 + dt]) for dt in range(3)]
@@ -118,11 +118,18 @@
     def _():
         side_copy(1).start()
 
-    for f in range(2):
-        loads[3 - f].wait()
-        taps(own, f, OWN[f])
-        conv_in[f] = joined(own, f, pl.ds(80, 320), 320)
-    loads[1].wait()
+    for i in (1, 2, 3):
+        loads[i].wait()
+
+    def own_part():
+        for f in range(2):
+            taps(own, f, OWN[f])
+            conv_in[f] = joined(own, f, pl.ds(80, 320), 320)
+
+    @pl.when(zl == 3)
+    def _():
+        own_part()
+
     for f in (1, 0):
         taps(nxt, f, NEXT[f])
         zin_out[f] = joined(nxt, f, pl.ds(80, 320), 320).astype(BF16).reshape(4, 80, 256)
@@ -164,6 +171,10 @@
     edge_next(near_side)
 
     edge_next(far_side)
+
+    @pl.when(zl != 3)
+    def _():
+        own_part()
 
     def edge_own(side, carry):
         dh = 2 * side

time: 54.8 us -> 55.2 us (level)
  no operation moved by 1% of the time
where the time goes in v7:
time: 55.2 us; the launch traced here: 55.1 us
  Pallas kernels  54.5 us (99%)
  between operations  0.64 us (1%)
    pallas_call x1, Pallas kernels, on_device(): pl.pallas_call(layer_kernel, out_shape=(jax.ShapeDtypeStruct((2, 6, 80, 2...  53.5 us

profile of v7, /device:TPU:1, one launch (start us, length us, event | category | flops | bytes accessed | tf_op | source)
XLA Modules:
  0.0 55.1 jit_solution(1607588459482284962)
XLA Ops:
  0.6 53.5 %shard_map.67 = (bf16[2,6,80,256]{3,2,1,0:T(8,128)(2,1)S(1)}, f32[640,128]{1,0:T(8,128)S(1)}) custom-call(bf16[2,6,80,256]{3,2,1,0:T(8,128)(2,1)} %lat_hbm.1, bf16[3,3,768,256]{3,2,1,0:T(8,128)(2,1)} %w_hbm.1, f32[256]{0:T(256)} %gain_hbm.1, bf16[2,6,80,128]{3,2,1,0:T(8,128)(2,1)} %tgt_hbm.1), custom_call_target="tpu_custom_call" | custom-call | tf_op jit(solution)/shard_map/pallas_call | solution.py:343
  54.2 0.9 %shard_map.68 = (bf16[2,6,80,256]{3,2,1,0:T(8,128)(2,1)}, f32[256,256]{1,0:T(8,128)}, f32[256,128]{1,0:T(8,128)}) custom-call(bf16[2,6,80,256]{3,2,1,0:T(8,128)(2,1)S(1)} %get-tuple-element.5.feat, f32[640,128]{1,0:T(8,128)S(1)} %get-tuple-element.6.fin), custom_call_target="tpu_custom_call" | custom-call | tf_op jit(solution)/shard_map/pallas_call | solution.py:381

commit v8 on v6

--- a/solution.py
+++ b/solution.py
@@ -186,16 +186,58 @@
     loads[4].wait()
     loads[5].wait()
 
-    def finish(conv, base, target, first):
+    def copy(stage, me, peer, k, src, dst):
+        j = (me + k) % 8
+        return pltpu.make_async_remote_copy(
+            src_ref=src(j), dst_ref=dst(me), send_sem=send_sem.at[stage, j], recv_sem=recv_sem.at[stage, me],
+            device_id=peer(j), device_id_type=MESH,
+        )
+
+    def arrival(stage, me, peer, k, src, dst):
+        j = (me + k) % 8
+        return pltpu.make_async_remote_copy(
+            src_ref=src(j), dst_ref=dst(j), send_sem=send_sem.at[stage, j], recv_sem=recv_sem.at[stage, j],
+            device_id=peer(j), device_id_type=MESH,
+        )
+
+    def send(stage, me, peer, src, dst):
+        for k in FAR:
+            copy(stage, me, peer, k, src, dst).start()
+
+    def receive(stage, me, peer, src, dst):
+        for k in FAR:
+            arrival(stage, me, peer, k, src, dst).wait_recv()
+
+    def drain(stage, me, peer, src, dst):
+        for k in FAR:
+            copy(stage, me, peer, k, src, dst).wait_send()
+
+    def chunk(ref, size):
+        return lambda j: ref.at[pl.ds(pl.multiple_of(j * size, 8), size)]
+
+    def slot(ref):
+        return lambda j: ref.at[j]
+
+    def total(ref):
+        acc = ref[0].astype(F32)
+        for j in range(1, 8):
+            acc = acc + ref[j].astype(F32)
+        return acc
+
+    s1 = (1, a_me, a_peer, lambda j: sums.at[pl.ds(pl.multiple_of(384 + j * 32, 8), 32)], slot(crs))
+
+    def finish(conv, base, target, first, last=False):
         size = conv.shape[0]
         mean = jnp.mean(conv * conv, axis=1, keepdims=True)
         v = conv * lax.rsqrt(mean + 1e-06) * gain_ref[...][None, :]
         out = (base.reshape(size, 256).astype(F32) + v / (1.0 + jnp.exp(-v))).astype(BF16)
         dims = (((0,), (0,)), ((), ()))
+        c = lax.dot_general(out, target.reshape(size, 128), dims, preferred_element_type=F32)
+        sums[384:640] = c if first else sums[384:640] + c
+        if last:
+            send(*s1)
         g = lax.dot_general(out, out, dims, preferred_element_type=F32)
-        c = lax.dot_general(out, target.reshape(size, 128), dims, preferred_element_type=F32)
-        blocks = (g[0:128, 0:128], g[0:128, 128:256], g[128:256, 128:256], c[0:128], c[128:256])
-        for i, block in enumerate(blocks):
+        for i, block in enumerate((g[0:128, 0:128], g[0:128, 128:256], g[128:256, 128:256])):
             place = slice(128 * i, 128 * i + 128)
             sums[place] = block if first else sums[place] + block
         return out
@@ -207,60 +249,20 @@
 
         conv = conv_in[f] + zin[f].reshape(320, 256).astype(F32)
         feat[f, 1:5] = finish(conv, win[f, 2:6], tgt[f, 1:5], f == 1).reshape(4, 80, 256)
-    for side in (near_side, far_side):
+    for last, side in ((False, near_side), (True, far_side)):
         @pl.when(has_prev)
         def _():
             edge_copy(side).wait_recv()
 
         conv = (conv_edge[side] + zed[side].astype(F32)).reshape(160, 256)
-        out = finish(conv, win[:, 1 + 5 * side], tgt[:, 5 * side], False)
+        out = finish(conv, win[:, 1 + 5 * side], tgt[:, 5 * side], False, last)
         feat[:, 5 * side] = out.reshape(2, 80, 256)
-
-    def copy(stage, me, peer, k, src, dst):
-        j = (me + k) % 8
-        return pltpu.make_async_remote_copy(
-            src_ref=src(j), dst_ref=dst(me), send_sem=send_sem.at[stage, j], recv_sem=recv_sem.at[stage, me],
-            device_id=peer(j), device_id_type=MESH,
-        )
-
-    def arrival(stage, me, peer, k, src, dst):
-        j = (me + k) % 8
-        return pltpu.make_async_remote_copy(
-            src_ref=src(j), dst_ref=dst(j), send_sem=send_sem.at[stage, j], recv_sem=recv_sem.at[stage, j],
-            device_id=peer(j), device_id_type=MESH,
-        )
-
-    def send(stage, me, peer, src, dst):
-        for k in FAR:
-            copy(stage, me, peer, k, src, dst).start()
-
-    def receive(stage, me, peer, src, dst):
-        for k in FAR:
-            arrival(stage, me, peer, k, src, dst).wait_recv()
-
-    def drain(stage, me, peer, src, dst):
-        for k in FAR:
-            copy(stage, me, peer, k, src, dst).wait_send()
-
-    def chunk(ref, size):
-        return lambda j: ref.at[pl.ds(pl.multiple_of(j * size, 8), size)]
-
-    def slot(ref):
-        return lambda j: ref.at[j]
-
-    def total(ref):
-        acc = ref[0].astype(F32)
-        for j in range(1, 8):
-            acc = acc + ref[j].astype(F32)
-        return acc
 
     gpay[...] = sums[0:384].astype(BF16)
     gplace = pl.ds(pl.multiple_of(a_me * 48, 16), 48)
     cplace = pl.ds(pl.multiple_of(384 + a_me * 32, 8), 32)
     s0 = (0, a_me, a_peer, chunk(gpay, 48), slot(grs))
-    s1 = (1, a_me, a_peer, lambda j: sums.at[pl.ds(pl.multiple_of(384 + j * 32, 8), 32)], slot(crs))
     send(*s0)
-    send(*s1)
     grs[a_me] = gpay[gplace]
     crs[a_me] = sums[cplace]
     receive(*s0)

time: 54.8 us -> 55.6 us (1.015)
  Pallas kernels: 54.1 us -> 54.9 us
    pallas_call x1, Pallas kernels: 53.1 us -> 53.9 us  [on_device(): pl.pallas_call(layer_kernel, out_shape=(jax.ShapeDtypeStruct((2, 6, 80, 2...]
where the time goes in v8:
time: 55.6 us; the launch traced here: 55.5 us
  Pallas kernels  54.9 us (99%)
  between operations  0.64 us (1%)
    pallas_call x1, Pallas kernels, on_device(): pl.pallas_call(layer_kernel, out_shape=(jax.ShapeDtypeStruct((2, 6, 80, 2...  53.9 us

profile of v8, /device:TPU:1, one launch (start us, length us, event | category | flops | bytes accessed | tf_op | source)
XLA Modules:
  0.0 55.5 jit_solution(14524223522729796819)
XLA Ops:
  0.6 53.9 %shard_map.67 = (bf16[2,6,80,256]{3,2,1,0:T(8,128)(2,1)S(1)}, f32[640,128]{1,0:T(8,128)S(1)}) custom-call(bf16[2,6,80,256]{3,2,1,0:T(8,128)(2,1)} %lat_hbm.1, bf16[3,3,768,256]{3,2,1,0:T(8,128)(2,1)} %w_hbm.1, f32[256]{0:T(256)} %gain_hbm.1, bf16[2,6,80,128]{3,2,1,0:T(8,128)(2,1)} %tgt_hbm.1), custom_call_target="tpu_custom_call" | custom-call | tf_op jit(solution)/shard_map/pallas_call | solution.py:334
  54.6 0.9 %shard_map.68 = (bf16[2,6,80,256]{3,2,1,0:T(8,128)(2,1)}, f32[256,256]{1,0:T(8,128)}, f32[256,128]{1,0:T(8,128)}) custom-call(bf16[2,6,80,256]{3,2,1,0:T(8,128)(2,1)S(1)} %get-tuple-element.5.feat, f32[640,128]{1,0:T(8,128)S(1)} %get-tuple-element.6.fin), custom_call_target="tpu_custom_call" | custom-call | tf_op jit(solution)/shard_map/pallas_call | solution.py:372
